TPU v7x, 32 devices: a whole 2x2x4 slice. The times are simulated.
32 devices in a mesh: rep: 8 (over y, x, core), grp: 4 (over z).
Axes of the slice: x: 2, y: 2, z: 4, core: 2. Of those that a mesh axis runs over, the one named last changes fastest.
Arguments:
- tokens: bfloat16 [16, 1024, 1024], P('rep', 'grp'), may hold values from -6 to 6
- positions: int32 [3, 16, 1024], P(None, 'rep', 'grp'), may hold values from 0 to 15
- ln1_gain: bfloat16 [1024], P('grp'), may hold values from 0.099609375 to 1.8984375
- ln1_bias: bfloat16 [1024], P('grp'), may hold values from -3 to 3
- w_qkv: bfloat16 [1024, 3072], P('grp'), may hold values from -0.1875 to 0.1875
- b_qkv: bfloat16 [3072], P('grp'), may hold values from -3 to 3
- w_out: bfloat16 [1024, 1024], P('grp'), may hold values from -0.75 to 0.75
- b_out: bfloat16 [1024], P('grp'), may hold values from -3 to 3
- ln2_gain: bfloat16 [1024], P('grp'), may hold values from 0.099609375 to 1.8984375
- ln2_bias: bfloat16 [1024], P('grp'), may hold values from -3 to 3
- w_up: bfloat16 [1024, 4096], P('grp'), may hold values from -0.1875 to 0.1875
- b_up: bfloat16 [4096], P('grp'), may hold values from -3 to 3
- w_down: bfloat16 [4096, 1024], P('grp'), may hold values from -0.09375 to 0.09375
- b_down: bfloat16 [1024], P('grp'), may hold values from -3 to 3
- cotangent: bfloat16 [16, 1024, 1024], P('rep', 'grp'), may hold values from -6 to 6
Outputs:
- output: bfloat16 [16, 1024, 1024], P('rep', 'grp')
- grad_tokens: bfloat16 [16, 1024, 1024], P('rep', 'grp')
- grad_ln1_gain: float32 [1024], P('grp')
- grad_ln1_bias: float32 [1024], P('grp')
- grad_w_qkv: float32 [1024, 3072], P('grp')
- grad_b_qkv: float32 [3072], P('grp')
- grad_w_out: float32 [1024, 1024], P('grp')
- grad_b_out: float32 [1024], P('grp')
- grad_ln2_gain: float32 [1024], P('grp')
- grad_ln2_bias: float32 [1024], P('grp')
- grad_w_up: float32 [1024, 4096], P('grp')
- grad_b_up: float32 [4096], P('grp')
- grad_w_down: float32 [4096, 1024], P('grp')
- grad_b_down: float32 [1024], P('grp')
Inputs may be any that keep to these rules, and one draw needn't show every extreme that they name: `positions`: frame, row and column indices of a token.
All inputs are finite; a program needn't handle non-finite values.
Results may differ from a plain program's by a relative error of at most 0.02.
Values may be sent and summed in bfloat16 or wider, within the bound.
A program may use at most 320 MiB of HBM per device.

v0:
```python
import jax
import jax.numpy as jnp
from jax import lax
from jax.sharding import PartitionSpec as P

SCALE = 0.125
EPS = 1e-06


def rotary_angles(positions):
    pair = jnp.arange(32)
    band = (pair >= 10).astype(jnp.int32) + (pair >= 21).astype(jnp.int32)
    start = jnp.where(band == 0, 0, jnp.where(band == 1, 10, 21))
    count = jnp.where(band == 0, 10, 11)
    freq = jnp.power(
        jnp.float32(10000.0), -(pair - start).astype(jnp.float32) / count.astype(jnp.float32)
    )
    pos_f = positions.astype(jnp.float32)
    chosen = jnp.where(
        band[None, :] == 0,
        pos_f[0][:, None],
        jnp.where(band[None, :] == 1, pos_f[1][:, None], pos_f[2][:, None]),
    )
    return chosen * freq[None, :]


def rotate(field, cosine, sine):
    first = field[..., :32]
    second = field[..., 32:]
    return jnp.concatenate(
        [first * cosine - second * sine, first * sine + second * cosine], axis=-1
    )


def normalize(field):
    centred = field - jnp.mean(field, axis=-1, keepdims=True)
    variance = jnp.mean(centred * centred, axis=-1, keepdims=True)
    factor = lax.rsqrt(variance + EPS)
    return (centred * factor, factor)


def norm_back(grad_norm, normed, factor):
    return factor * (
        grad_norm
        - jnp.mean(grad_norm, axis=-1, keepdims=True)
        - normed * jnp.mean(grad_norm * normed, axis=-1, keepdims=True)
    )


def outer(left, right):
    return lax.dot_general(
        left, right, (((0,), (0,)), ((), ())), preferred_element_type=jnp.float32
    )


def back(left, right):
    return lax.dot_general(
        left, right, (((1,), (1,)), ((), ())), preferred_element_type=jnp.float32
    )


def exact_gelu(value):
    return jax.nn.gelu(value, approximate=False)


def column_sum(value):
    return jnp.sum(value.astype(jnp.float32), axis=0)


def forward_pass(params, field_in, positions):
    g1, b1, wqkv, bqkv, wo, bo, g2, b2, w1, bu, w2, bd = params
    field = field_in.astype(jnp.float32)
    count, width = field.shape
    heads = width // 64
    angles = rotary_angles(positions)
    cosine = jnp.cos(angles)[:, None, :]
    sine = jnp.sin(angles)[:, None, :]
    normed1, factor1 = normalize(field)
    h1 = (normed1 * g1.astype(jnp.float32) + b1.astype(jnp.float32)).astype(jnp.bfloat16)
    qkv = jnp.dot(h1, wqkv, preferred_element_type=jnp.float32) + bqkv.astype(jnp.float32)
    query_rot = rotate(qkv[:, :width].reshape(count, heads, 64), cosine, sine).astype(jnp.bfloat16)
    keys_rot = (
        rotate(qkv[:, width : 2 * width].reshape(count, heads, 64), cosine, sine)
        .astype(jnp.bfloat16)
        .reshape(count, width)
    )
    values = qkv[:, 2 * width :].astype(jnp.bfloat16)
    keys_all, values_all = (
        lax.all_gather(keys_rot, "grp", axis=0, tiled=True),
        lax.all_gather(values, "grp", axis=0, tiled=True),
    )
    total = keys_all.shape[0]
    keys_all = keys_all.reshape(total, heads, 64)
    values_all = values_all.reshape(total, heads, 64)
    scores = (
        jnp.einsum("thd,shd->hts", query_rot, keys_all, preferred_element_type=jnp.float32) * SCALE
    )
    top = jnp.max(scores, axis=-1, keepdims=True)
    lse = top + jnp.log(jnp.sum(jnp.exp(scores - top), axis=-1, keepdims=True))
    probs = jnp.exp(scores - lse).astype(jnp.bfloat16)
    mixed = (
        jnp.einsum("hts,shd->thd", probs, values_all, preferred_element_type=jnp.float32)
        .reshape(count, width)
        .astype(jnp.bfloat16)
    )
    second = field + jnp.dot(mixed, wo, preferred_element_type=jnp.float32) + bo.astype(jnp.float32)
    normed2, factor2 = normalize(second)
    h2 = (normed2 * g2.astype(jnp.float32) + b2.astype(jnp.float32)).astype(jnp.bfloat16)
    hidden = jnp.dot(h2, w1, preferred_element_type=jnp.float32) + bu.astype(jnp.float32)
    active = exact_gelu(hidden).astype(jnp.bfloat16)
    result = (
        second + jnp.dot(active, w2, preferred_element_type=jnp.float32) + bd.astype(jnp.float32)
    )
    saved = (
        normed1,
        factor1,
        h1,
        query_rot,
        keys_rot,
        values,
        lse,
        mixed,
        normed2,
        factor2,
        h2,
        hidden,
        active,
        cosine,
        sine,
    )
    return (saved, result.astype(jnp.bfloat16))


def backward_pass(params, saved, grad_in, totals):
    g1, b1, wqkv, bqkv, wo, bo, g2, b2, w1, bu, w2, bd = params
    (
        normed1,
        factor1,
        h1,
        query_rot,
        keys_rot,
        values,
        lse,
        mixed,
        normed2,
        factor2,
        h2,
        hidden,
        active,
        cosine,
        sine,
    ) = saved
    grad_out = grad_in.astype(jnp.float32)
    count, width = grad_out.shape
    heads = width // 64
    grad_y2 = grad_out.astype(jnp.bfloat16)
    grad_w2 = outer(active, grad_y2)
    grad_bd = column_sum(grad_y2)
    grad_act = back(grad_y2, w2)
    unused, pull = jax.vjp(exact_gelu, hidden)
    grad_hidden = pull(grad_act)[0].astype(jnp.bfloat16)
    grad_w1 = outer(h2, grad_hidden)
    grad_bu = column_sum(grad_hidden)
    grad_h2 = back(grad_hidden, w1)
    grad_g2 = jnp.sum(grad_h2 * normed2, axis=0)
    grad_b2 = jnp.sum(grad_h2, axis=0)
    grad_second = grad_out + norm_back(grad_h2 * g2.astype(jnp.float32), normed2, factor2)
    grad_y1 = grad_second.astype(jnp.bfloat16)
    grad_wo = outer(mixed, grad_y1)
    grad_bo = column_sum(grad_y1)
    grad_mixed = back(grad_y1, wo).astype(jnp.bfloat16).reshape(count, heads, 64)
    keys_all, values_all = (
        lax.all_gather(keys_rot, "grp", axis=0, tiled=True),
        lax.all_gather(values, "grp", axis=0, tiled=True),
    )
    total = keys_all.shape[0]
    keys_all = keys_all.reshape(total, heads, 64)
    values_all = values_all.reshape(total, heads, 64)
    scores = (
        jnp.einsum("thd,shd->hts", query_rot, keys_all, preferred_element_type=jnp.float32) * SCALE
    )
    probs = jnp.exp(scores - lse)
    grad_probs = jnp.einsum(
        "thd,shd->hts", grad_mixed, values_all, preferred_element_type=jnp.float32
    )
    delta = jnp.sum(probs * grad_probs, axis=-1, keepdims=True)
    grad_scores = (probs * (grad_probs - delta)).astype(jnp.bfloat16)
    grad_query = (
        jnp.einsum("hts,shd->thd", grad_scores, keys_all, preferred_element_type=jnp.float32)
        * SCALE
    )
    probs_low = probs.astype(jnp.bfloat16)
    grad_values = jnp.einsum(
        "hts,thd->shd", probs_low, grad_mixed, preferred_element_type=jnp.float32
    )
    grad_keys = (
        jnp.einsum("hts,thd->shd", grad_scores, query_rot, preferred_element_type=jnp.float32)
        * SCALE
    )
    keys_own, values_own = (
        lax.psum_scatter(
            grad_keys.reshape(total, width).astype(jnp.bfloat16),
            "grp",
            scatter_dimension=0,
            tiled=True,
        ).astype(jnp.float32),
        lax.psum_scatter(
            grad_values.reshape(total, width).astype(jnp.bfloat16),
            "grp",
            scatter_dimension=0,
            tiled=True,
        ).astype(jnp.float32),
    )
    query_back = rotate(grad_query, cosine, -sine).reshape(count, width)
    keys_back = rotate(keys_own.reshape(count, heads, 64), cosine, -sine).reshape(count, width)
    grad_qkv = jnp.concatenate([query_back, keys_back, values_own], axis=1).astype(jnp.bfloat16)
    grad_wqkv = outer(h1, grad_qkv)
    grad_bqkv = column_sum(grad_qkv)
    grad_h1 = back(grad_qkv, wqkv)
    grad_g1 = jnp.sum(grad_h1 * normed1, axis=0)
    grad_b1 = jnp.sum(grad_h1, axis=0)
    grad_field = grad_second + norm_back(grad_h1 * g1.astype(jnp.float32), normed1, factor1)
    terms = (
        grad_g1,
        grad_b1,
        grad_wqkv,
        grad_bqkv,
        grad_wo,
        grad_bo,
        grad_g2,
        grad_b2,
        grad_w1,
        grad_bu,
        grad_w2,
        grad_bd,
    )
    totals = tuple((a + b for a, b in zip(totals, terms)))
    return (grad_field.astype(jnp.bfloat16), totals)


def local(
    tokens,
    positions,
    ln1_gain,
    ln1_bias,
    w_qkv,
    b_qkv,
    w_out,
    b_out,
    ln2_gain,
    ln2_bias,
    w_up,
    b_up,
    w_down,
    b_down,
    cotangent,
):
    shards = (
        ln1_gain,
        ln1_bias,
        w_qkv,
        b_qkv,
        w_out,
        b_out,
        ln2_gain,
        ln2_bias,
        w_up,
        b_up,
        w_down,
        b_down,
    )
    groups = lax.axis_size("grp")
    totals = tuple((jnp.zeros((s.shape[0] * groups,) + s.shape[1:], jnp.float32) for s in shards))
    outputs = []
    gradients = []
    for index in range(tokens.shape[0]):
        forward_params = (
            lax.all_gather(ln1_gain, "grp", axis=0, tiled=True),
            lax.all_gather(ln1_bias, "grp", axis=0, tiled=True),
            lax.all_gather(w_qkv, "grp", axis=0, tiled=True),
            lax.all_gather(b_qkv, "grp", axis=0, tiled=True),
            lax.all_gather(w_out, "grp", axis=0, tiled=True),
            lax.all_gather(b_out, "grp", axis=0, tiled=True),
            lax.all_gather(ln2_gain, "grp", axis=0, tiled=True),
            lax.all_gather(ln2_bias, "grp", axis=0, tiled=True),
            lax.all_gather(w_up, "grp", axis=0, tiled=True),
            lax.all_gather(b_up, "grp", axis=0, tiled=True),
            lax.all_gather(w_down, "grp", axis=0, tiled=True),
            lax.all_gather(b_down, "grp", axis=0, tiled=True),
        )
        saved, result = forward_pass(forward_params, tokens[index], positions[:, index, :])
        outputs.append(result)
        backward_params = (
            lax.all_gather(ln1_gain, "grp", axis=0, tiled=True),
            lax.all_gather(ln1_bias, "grp", axis=0, tiled=True),
            lax.all_gather(w_qkv, "grp", axis=0, tiled=True),
            lax.all_gather(b_qkv, "grp", axis=0, tiled=True),
            lax.all_gather(w_out, "grp", axis=0, tiled=True),
            lax.all_gather(b_out, "grp", axis=0, tiled=True),
            lax.all_gather(ln2_gain, "grp", axis=0, tiled=True),
            lax.all_gather(ln2_bias, "grp", axis=0, tiled=True),
            lax.all_gather(w_up, "grp", axis=0, tiled=True),
            lax.all_gather(b_up, "grp", axis=0, tiled=True),
            lax.all_gather(w_down, "grp", axis=0, tiled=True),
            lax.all_gather(b_down, "grp", axis=0, tiled=True),
        )
        grad_field, totals = backward_pass(backward_params, saved, cotangent[index], totals)
        gradients.append(grad_field)
    owned = (
        lax.psum_scatter(
            totals[0].astype(jnp.bfloat16), "grp", scatter_dimension=0, tiled=True
        ).astype(jnp.float32),
        lax.psum_scatter(
            totals[1].astype(jnp.bfloat16), "grp", scatter_dimension=0, tiled=True
        ).astype(jnp.float32),
        lax.psum_scatter(
            totals[2].astype(jnp.bfloat16), "grp", scatter_dimension=0, tiled=True
        ).astype(jnp.float32),
        lax.psum_scatter(
            totals[3].astype(jnp.bfloat16), "grp", scatter_dimension=0, tiled=True
        ).astype(jnp.float32),
        lax.psum_scatter(
            totals[4].astype(jnp.bfloat16), "grp", scatter_dimension=0, tiled=True
        ).astype(jnp.float32),
        lax.psum_scatter(
            totals[5].astype(jnp.bfloat16), "grp", scatter_dimension=0, tiled=True
        ).astype(jnp.float32),
        lax.psum_scatter(
            totals[6].astype(jnp.bfloat16), "grp", scatter_dimension=0, tiled=True
        ).astype(jnp.float32),
        lax.psum_scatter(
            totals[7].astype(jnp.bfloat16), "grp", scatter_dimension=0, tiled=True
        ).astype(jnp.float32),
        lax.psum_scatter(
            totals[8].astype(jnp.bfloat16), "grp", scatter_dimension=0, tiled=True
        ).astype(jnp.float32),
        lax.psum_scatter(
            totals[9].astype(jnp.bfloat16), "grp", scatter_dimension=0, tiled=True
        ).astype(jnp.float32),
        lax.psum_scatter(
            totals[10].astype(jnp.bfloat16), "grp", scatter_dimension=0, tiled=True
        ).astype(jnp.float32),
        lax.psum_scatter(
            totals[11].astype(jnp.bfloat16), "grp", scatter_dimension=0, tiled=True
        ).astype(jnp.float32),
    )
    summed = (
        lax.psum(owned[0].astype(jnp.bfloat16), "rep").astype(jnp.float32),
        lax.psum(owned[1].astype(jnp.bfloat16), "rep").astype(jnp.float32),
        lax.psum(owned[2].astype(jnp.bfloat16), "rep").astype(jnp.float32),
        lax.psum(owned[3].astype(jnp.bfloat16), "rep").astype(jnp.float32),
        lax.psum(owned[4].astype(jnp.bfloat16), "rep").astype(jnp.float32),
        lax.psum(owned[5].astype(jnp.bfloat16), "rep").astype(jnp.float32),
        lax.psum(owned[6].astype(jnp.bfloat16), "rep").astype(jnp.float32),
        lax.psum(owned[7].astype(jnp.bfloat16), "rep").astype(jnp.float32),
        lax.psum(owned[8].astype(jnp.bfloat16), "rep").astype(jnp.float32),
        lax.psum(owned[9].astype(jnp.bfloat16), "rep").astype(jnp.float32),
        lax.psum(owned[10].astype(jnp.bfloat16), "rep").astype(jnp.float32),
        lax.psum(owned[11].astype(jnp.bfloat16), "rep").astype(jnp.float32),
    )
    output = jnp.stack(outputs, axis=0)
    grad_tokens = jnp.stack(gradients, axis=0)
    return (
        output,
        grad_tokens,
        summed[0],
        summed[1],
        summed[2],
        summed[3],
        summed[4],
        summed[5],
        summed[6],
        summed[7],
        summed[8],
        summed[9],
        summed[10],
        summed[11],
    )


def solution(mesh):
    placed = (
        P("rep", "grp", None),
        P(None, "rep", "grp"),
        P("grp"),
        P("grp"),
        P("grp", None),
        P("grp"),
        P("grp", None),
        P("grp"),
        P("grp"),
        P("grp"),
        P("grp", None),
        P("grp"),
        P("grp", None),
        P("grp"),
        P("rep", "grp", None),
    )
    return jax.shard_map(
        local,
        mesh=mesh,
        in_specs=placed,
        out_specs=(
            P("rep", "grp", None),
            P("rep", "grp", None),
            P("grp"),
            P("grp"),
            P("grp", None),
            P("grp"),
            P("grp", None),
            P("grp"),
            P("grp"),
            P("grp"),
            P("grp", None),
            P("grp"),
            P("grp", None),
            P("grp"),
        ),
        check_vma=False,
    )
```

profile of v0, /device:TPU:0, one launch (start us, length us, event | category | flops | bytes accessed | tf_op | source)
XLA Modules:
  0.0 1496.7 jit_solution(1610655362138257316)
XLA Ops:
  8.6 14.8 all-gather.2
  24.2 12.4 all-gather.1
  37.3 8.0 all-gather
  50.1 77.6 %all-gather.16.cloned.1.call-done = bf16[1024,3072]{1,0:T(8,128)(2,1)} async-done(((bf16[256,3072]{1,0:T(8,128)(2,1)}), bf16[1024,3072]{1,0:T(8,128)(2,1)}) %all-gather.16.cloned.1.call-update) | async-done | bytes 6291472 | tf_op jit(solution)/shard_map/all_gather | solution.py:280
  127.8 4.9 convolution_add_fusion.2
  140.9 4.8 convolution_add_fusion.3
  157.1 8.3 all-gather.3
  165.4 15.3 %all_gather.43 = bf16[4096]{0:T(1024)(128)(2,1)S(1)} all-gather(bf16[1024]{0:T(1024)(128)(2,1)S(1)} %copy-done.99), channel_id=1, replica_groups=mesh['rep'=8,'grp'=4] {'grp'}, dimensions={0}, use_global_device_ids=true | all-gather | bytes 10240 | tf_op jit(solution)/shard_map/all_gather | solution.py:287
  181.4 11.2 all-gather.5
  192.6 8.3 all-gather.4
  200.9 4.1 multiply_reduce_fusion.2
  205.0 5.8 copy-done
  210.8 3.6 exponential_reduce_fusion
  214.4 15.0 %all-gather.28.cloned.1.call-done = bf16[1024,1024]{1,0:T(8,128)(2,1)} async-done(((bf16[256,1024]{1,0:T(8,128)(2,1)}), bf16[1024,1024]{1,0:T(8,128)(2,1)}) %all-gather.28.cloned.1.call-update) | async-done | bytes 2097168 | tf_op jit(solution)/shard_map/all_gather | solution.py:90
  229.4 2.9 copy.56
  232.3 43.6 %all-gather.18.cloned.1.call-done = bf16[1024,1024]{1,0:T(8,128)(2,1)} async-done(((bf16[256,1024]{1,0:T(8,128)(2,1)}), bf16[1024,1024]{1,0:T(8,128)(2,1)}) %all-gather.18.cloned.1.call-update) | async-done | bytes 2097168 | tf_op jit(solution)/shard_map/all_gather | solution.py:90
  275.9 3.9 copy.53
  280.5 8.7 convolution_convert_fusion.2
  289.2 32.7 %all-gather.22.cloned.1.call-done = bf16[1024,1024]{1,0:T(8,128)(2,1)} async-done(((bf16[256,1024]{1,0:T(8,128)(2,1)}), bf16[1024,1024]{1,0:T(8,128)(2,1)}) %all-gather.22.cloned.1.call-update) | async-done | bytes 2097168 | tf_op jit(solution)/shard_map/all_gather | solution.py:282
  325.7 43.2 %all-gather.20.cloned.1.call-done = bf16[1024,1024]{0,1:T(8,128)(2,1)} async-done(((bf16[256,1024]{0,1:T(8,128)(2,1)}), bf16[1024,1024]{0,1:T(8,128)(2,1)}) %all-gather.20.cloned.1.call-update) | async-done | bytes 2097168 | tf_op jit(solution)/shard_map/all_gather | solution.py:89
  368.9 4.1 multiply_reduce_fusion.3
  373.0 3.6 exponential_reduce_fusion.1
  376.7 4.2 copy-done.1
  380.9 3.8 convolution_convert_fusion.3
  386.8 131.5 %all-gather.24.cloned.1.call-done = bf16[1024,4096]{1,0:T(8,128)(2,1)} async-done(((bf16[256,4096]{1,0:T(8,128)(2,1)}), bf16[1024,4096]{1,0:T(8,128)(2,1)}) %all-gather.24.cloned.1.call-update) | async-done | bytes 8388624 | tf_op jit(solution)/shard_map/all_gather | solution.py:286
  518.3 17.5 %multiply_convert_fusion.4 = (bf16[256,4096]{1,0:T(8,128)(2,1)}, f32[256,4096]{1,0:T(8,128)}, f32[256,4096]{1,0:T(8,128)}) fusion(f32[4096]{0:T(1024)} %convert_element_type.404, bf16[1024,4096]{1,0:T(8,128)(2,1)} %all-gather.24.cloned.1.call-done, f32[256,1024]{1,0:T(8,128)} %copy-done.16, f32[256]{0:T(256)S(1)} %add_rsqrt_fusion, f32[256]{0:T(256)} %copy-done.89, ...), kind=kOutput, calls=%fused_computation.28 | convolution fusion | flops 2218000384 | bytes 19949568 | tf_op jit(solution)/shard_map/dot_general | solution.py:109
  535.8 16.7 %multiply_convert_fusion.5 = (bf16[256,4096]{1,0:T(8,128)(2,1)}, f32[256,4096]{1,0:T(8,128)}, f32[256,4096]{1,0:T(8,128)}) fusion(f32[4096]{0:T(1024)S(1)} %copy-done.83, bf16[1024,4096]{1,0:T(8,128)(2,1)S(1)} %copy-done.100, f32[256,1024]{1,0:T(8,128)S(1)} %copy-done.11, f32[1024]{0:T(1024)S(1)} %bitcast.273, f32[1024]{0:T(1024)S(1)} %bitcast.267, ...), kind=kOutput, calls=%fused_computation.41 | convolution fusion | flops 2218000384 | bytes 19949568 | tf_op jit(solution)/shard_map/dot_general | solution.py:109
  552.5 115.2 %all-gather.26.cloned.1.call-done = bf16[4096,1024]{1,0:T(8,128)(2,1)} async-done(((bf16[1024,1024]{1,0:T(8,128)(2,1)}), bf16[4096,1024]{1,0:T(8,128)(2,1)}) %all-gather.26.cloned.1.call-update) | async-done | bytes 8388624 | tf_op jit(solution)/shard_map/all_gather | solution.py:288
  667.7 10.3 convert_reduce_fusion
  678.0 6.8 fusion.116
  684.9 11.9 convert_reduce_fusion.1
  696.8 8.0 multiply_reduce_fusion.5
  712.1 15.6 %multiply_reduce_fusion = (f32[16,256]{1,0:T(8,128)}, f32[16,256,1024]{2,1,0:T(8,128)}) fusion(f32[16,256,1024]{2,1,0:T(8,128)} %copy-done, f32[16,256]{1,0:T(8,128)} %copy-done.56, bf16[256,16,64]{0,2,1:T(8,128)(2,1)} %bitcast.234, bf16[1024,16,64]{0,2,1:T(8,128)(2,1)} %bitcast.219), kind=kOutput, calls=%fused_computation.3 | convolution fusion | flops 553644032 | bytes 36208640 | tf_op jit(solution)/shard_map/thd,shd->hts/dot_general | solution.py:183
  729.4 8.1 multiply_convert_fusion
  737.5 2.9 multiply_convert_fusion.2
  741.7 2.8 convolution_convert_fusion.5
  746.6 16.1 %multiply_reduce_fusion.1 = (f32[16,256]{1,0:T(8,128)}, f32[16,256,1024]{2,1,0:T(8,128)}) fusion(f32[16,256,1024]{2,1,0:T(8,128)} %copy-done.1, f32[16,256]{1,0:T(8,128)} %copy-done.58, bf16[256,16,64]{0,2,1:T(8,128)(2,1)} %bitcast.236, bf16[1024,16,64]{0,2,1:T(8,128)(2,1)} %bitcast.216), kind=kOutput, calls=%fused_computation.5 | convolution fusion | flops 553644032 | bytes 36208640 | tf_op jit(solution)/shard_map/thd,shd->hts/dot_general | solution.py:183
  763.9 8.2 multiply_convert_fusion.1
  772.1 3.4 multiply_convert_fusion.3
  776.1 9.4 convolution_convert_fusion.1
  785.6 9.6 convolution_convert_fusion
  799.6 7.9 fusion.14
  807.5 7.1 fusion.15
  815.7 12.9 reduce-scatter.9.cloned.1.call-done
  835.2 38.6 %reduce-scatter.11.cloned.1.call-done = bf16[256,1024]{0,1:T(8,128)(2,1)} async-done(((bf16[1024,1024]{0,1:T(8,128)(2,1)}), bf16[256,1024]{0,1:T(8,128)(2,1)}) %reduce-scatter.11.cloned.1.call-update) | async-done | bytes 524304 | tf_op jit(solution)/shard_map/reduce_scatter | solution.py:207
  873.8 8.0 fusion.100
  881.8 37.5 %reduce-scatter.15.cloned.1.call-done = bf16[256,1024]{0,1:T(8,128)(2,1)} async-done(((bf16[1024,1024]{0,1:T(8,128)(2,1)}), bf16[256,1024]{0,1:T(8,128)(2,1)}) %reduce-scatter.15.cloned.1.call-update) | async-done | bytes 524304 | tf_op jit(solution)/shard_map/reduce_scatter | solution.py:207
  919.4 9.9 add_convert_fusion.2
  929.9 10.1 fusion.107
  940.0 11.8 add_convert_fusion.1
  951.9 10.0 fusion.67
  961.9 12.3 add_convert_fusion
  974.8 11.6 all-gather.6
  989.0 6.8 fusion.36
  995.9 5.8 fusion.37
  1002.9 73.8 %reduce-scatter.17.cloned.1.call-done = bf16[256,3072]{1,0:T(8,128)(2,1)} async-done(((bf16[1024,3072]{1,0:T(8,128)(2,1)}), bf16[256,3072]{1,0:T(8,128)(2,1)}) %reduce-scatter.17.cloned.1.call-update) | async-done | bytes 1572880 | tf_op jit(solution)/shard_map/reduce_scatter | solution.py:316
  1076.7 147.4 %reduce-scatter.21.cloned.1.call-done = bf16[256,4096]{1,0:T(8,128)(2,1)} async-done(((bf16[1024,4096]{1,0:T(8,128)(2,1)}), bf16[256,4096]{1,0:T(8,128)(2,1)}) %reduce-scatter.21.cloned.1.call-update) | async-done | bytes 2097168 | tf_op jit(solution)/shard_map/reduce_scatter | solution.py:334
  1224.1 147.5 %reduce-scatter.23.cloned.1.call-done = bf16[1024,1024]{1,0:T(8,128)(2,1)} async-done(((bf16[4096,1024]{1,0:T(8,128)(2,1)}), bf16[1024,1024]{1,0:T(8,128)(2,1)}) %reduce-scatter.23.cloned.1.call-update) | async-done | bytes 2097168 | tf_op jit(solution)/shard_map/reduce_scatter | solution.py:340
  1371.7 4.9 fusion.105
  1377.7 6.3 fusion.58
  1384.1 18.4 %all-reduce.10 = (bf16[1024]{0:T(1024)(128)(2,1)S(1)}, bf16[1024]{0:T(1024)(128)(2,1)S(1)}, bf16[3072]{0:T(1024)(128)(2,1)S(1)}, bf16[1024]{0:T(1024)(128)(2,1)S...) all-reduce(bf16[1024]{0:T(1024)(128)(2,1)S(1)} %add_convert_fusion., ...), channel_id=6, replica_groups=mesh['rep'=8,'grp'=4] {'grp'}, use_global_device_ids=true, to_apply=%region_28.29.clone | all-reduce | flops 13312 | bytes 53248
  1403.0 12.3 all-reduce.8
  1423.3 56.7 %all-reduce.13.cloned.1.call-done = (bf16[256,3072]{1,0:T(8,128)(2,1)}, bf16[256,1024]{1,0:T(8,128)(2,1)}, bf16[256,4096]{1,0:T(8,128)(2,1)}, bf16[1024,1024]{1,0:T(8,128)(2,1)}) async-done(((bf16[256,3072]{1,0:T(8,128)(2,1)}, bf16[256,1024]{1,0:T(8,128)(2,1)}, bf16[256,4096]{1,0:T(8,128)(2,1)}, bf16[1024,1024]{1,0:T(8,128)(2,1)}), (bf16[256,3072]{1,0:T(8,128)(2,1)}, bf16[256,1024]{1,0:T(8,128)(2,1)}, ...) | async-done | bytes 6291472 | tf_op jit(solution)/shard_map/psum | solution.py:350
  1480.0 3.6 convert_element_type.449
  (369 shorter events, 78.8 us)
Async XLA Ops:
  7.2 120.6 %all-gather.16.cloned.1.call-start = ((), (), s32[]{:S(2)}) async-start(), calls=%async_computation.8 | async-start | bytes 7864320 | tf_op jit(solution)/shard_map/all_gather | solution.py:280
  7.9 193.0 %all-gather.30.cloned.1.call-start = ((), (), s32[]{:S(2)}) async-start(), calls=%async_computation.15 | async-start | bytes 2621440 | tf_op jit(solution)/shard_map/all_gather | solution.py:89
  23.5 109.2 %copy-start.92 = (f32[4,1,768]{2,1,0:T(1,128)}, f32[4,1,768]{2,1,0:T(1,128)S(1)}, u32[]{:S(2)}) copy-start(f32[4,1,768]{2,1,0:T(1,128)S(1)} %convert_element_type.476) | copy-start | bytes 36868
  36.6 104.3 %copy-start.54 = (f32[4,1,256]{2,1,0:T(1,128)}, f32[4,1,256]{2,1,0:T(1,128)S(1)}, u32[]{:S(2)}) copy-start(f32[4,1,256]{2,1,0:T(1,128)S(1)} %convert_element_type.475) | copy-start | bytes 12292
  45.3 95.6 %copy-start.51 = (f32[4,1,256]{2,1,0:T(1,128)}, f32[4,1,256]{2,1,0:T(1,128)S(1)}, u32[]{:S(2)}) copy-start(f32[4,1,256]{2,1,0:T(1,128)S(1)} %convert_element_type.474) | copy-start | bytes 12292
  46.7 85.9 %copy-start.71 = (f32[256]{0:T(256)}, f32[256]{0:T(256)S(1)}, u32[]{:S(2)}) copy-start(f32[256]{0:T(256)S(1)} %get-tuple-element.143) | copy-start | bytes 3076
  46.8 94.1 %copy-start.66 = (f32[256]{0:T(256)}, f32[256]{0:T(256)S(1)}, u32[]{:S(2)}) copy-start(f32[256]{0:T(256)S(1)} %get-tuple-element.144) | copy-start | bytes 3076
  48.4 84.3 %copy-start.86 = (f32[256]{0:T(256)}, f32[256]{0:T(256)S(1)}, u32[]{:S(2)}) copy-start(f32[256]{0:T(256)S(1)} %add_rsqrt_fusion.1) | copy-start | bytes 3076
  50.1 86.6 %copy-start.62 = (f32[256,32]{0,1:T(8,128)}, f32[256,32]{0,1:T(8,128)S(1)}, u32[]{:S(2)}) copy-start(f32[256,32]{0,1:T(8,128)S(1)} %get-tuple-element.121) | copy-start | bytes 98308
  50.1 103.4 %copy-start.60 = (f32[256,32]{0,1:T(8,128)}, f32[256,32]{0,1:T(8,128)S(1)}, u32[]{:S(2)}) copy-start(f32[256,32]{0,1:T(8,128)S(1)} %get-tuple-element.106) | copy-start | bytes 98308
  137.7 63.2 %copy-start.32 = (bf16[256,16,32]{0,2,1:T(8,128)(2,1)}, bf16[256,16,32]{0,2,1:T(8,128)(2,1)S(1)}, u32[]{:S(2)}) copy-start(bf16[256,16,32]{0,2,1:T(8,128)(2,1)S(1)} %get-tuple-element.82) | copy-start | bytes 786436
  138.6 90.8 %all-gather.28.cloned.1.call-start = ((), (), s32[]{:S(2)}) async-start(), calls=%async_computation.14 | async-start | bytes 2621440 | tf_op jit(solution)/shard_map/all_gather | solution.py:90
  140.8 135.1 %all-gather.18.cloned.1.call-start = ((), (), s32[]{:S(2)}) async-start(), calls=%async_computation.9 | async-start | bytes 2621440 | tf_op jit(solution)/shard_map/all_gather | solution.py:90
  148.3 173.6 %all-gather.22.cloned.1.call-start = ((), (), s32[]{:S(2)}) async-start(), calls=%async_computation.11 | async-start | bytes 2621440 | tf_op jit(solution)/shard_map/all_gather | solution.py:282
  148.9 220.0 %all-gather.20.cloned.1.call-start = ((), (), s32[]{:S(2)}) async-start(), calls=%async_computation.10 | async-start | bytes 2621440 | tf_op jit(solution)/shard_map/all_gather | solution.py:89
  153.6 27.8 %copy-start.102 = (bf16[256]{0:T(256)(128)(2,1)S(1)}, bf16[256]{0:T(256)(128)(2,1)}, u32[]{:S(2)}) copy-start(bf16[256]{0:T(256)(128)(2,1)} %param.24) | copy-start | bytes 1540
  153.6 39.0 %copy-start.103 = (bf16[256]{0:T(256)(128)(2,1)S(1)}, bf16[256]{0:T(256)(128)(2,1)}, u32[]{:S(2)}) copy-start(bf16[256]{0:T(256)(128)(2,1)} %param.23) | copy-start | bytes 1540
  154.7 46.2 %copy-start.34 = (bf16[256,16,32]{0,2,1:T(8,128)(2,1)S(1)}, bf16[256,16,32]{0,2,1:T(8,128)(2,1)}, u32[]{:S(2)}) copy-start(bf16[256,16,32]{0,2,1:T(8,128)(2,1)} %get-tuple-element.83) | copy-start | bytes 786436
  155.6 362.8 %all-gather.24.cloned.1.call-start = ((), (), s32[]{:S(2)}) async-start(), calls=%async_computation.12 | async-start | bytes 10485760 | tf_op jit(solution)/shard_map/all_gather | solution.py:286
  156.3 511.4 %all-gather.26.cloned.1.call-start = ((), (), s32[]{:S(2)}) async-start(), calls=%async_computation.13 | async-start | bytes 10485760 | tf_op jit(solution)/shard_map/all_gather | solution.py:288
  157.1 657.5 %reduce-scatter.13.cloned.1.call-start = ((), (), s32[]{:S(2)}) async-start(), calls=%async_computation.18 | async-start | bytes 2621440 | tf_op jit(solution)/shard_map/reduce_scatter | solution.py:201
  232.3 56.9 %copy-start.9 = (bf16[1024,1024]{0,1:T(8,128)(2,1)}, bf16[1024,1024]{0,1:T(8,128)(2,1)S(1)}, u32[]{:S(2)}) copy-start(bf16[1024,1024]{0,1:T(8,128)(2,1)S(1)} %copy.56) | copy-start | bytes 6291460
  289.2 79.8 %copy-start.36 = (bf16[256,16,32]{0,2,1:T(8,128)(2,1)S(1)}, bf16[256,16,32]{0,2,1:T(8,128)(2,1)}, u32[]{:S(2)}) copy-start(bf16[256,16,32]{0,2,1:T(8,128)(2,1)} %get-tuple-element.78) | copy-start | bytes 786436
  321.8 47.1 %copy-start.38 = (bf16[256,16,32]{0,2,1:T(8,128)(2,1)S(1)}, bf16[256,16,32]{0,2,1:T(8,128)(2,1)}, u32[]{:S(2)}) copy-start(bf16[256,16,32]{0,2,1:T(8,128)(2,1)} %get-tuple-element.79) | copy-start | bytes 786436
  324.5 44.4 %copy-start.89 = (f32[256]{0:T(256)}, f32[256]{0:T(256)S(1)}, u32[]{:S(2)}) copy-start(f32[256]{0:T(256)S(1)} %broadcast_multiply_fusion.8) | copy-start | bytes 3076
  385.5 319.4 %copy-start.69 = (f32[256]{0:T(256)}, f32[256]{0:T(256)S(1)}, u32[]{:S(2)}) copy-start(f32[256]{0:T(256)S(1)} %broadcast_multiply_fusion.10) | copy-start | bytes 3076
  386.7 318.1 %copy-start.93 = (f32[256]{0:T(256)}, f32[256]{0:T(256)S(1)}, u32[]{:S(2)}) copy-start(f32[256]{0:T(256)S(1)} %add_rsqrt_fusion) | copy-start | bytes 3076
  386.8 318.1 %copy-start.77 = (f32[256]{0:T(256)}, f32[256]{0:T(256)S(1)}, u32[]{:S(2)}) copy-start(f32[256]{0:T(256)S(1)} %add_rsqrt_fusion.2) | copy-start | bytes 3076
  518.3 17.5 %copy-start.11 = (f32[256,1024]{1,0:T(8,128)S(1)}, f32[256,1024]{1,0:T(8,128)}, u32[]{:S(2)}) copy-start(f32[256,1024]{1,0:T(8,128)} %copy-done.10) | copy-start | bytes 3145732
  518.3 17.5 %copy-start.83 = (f32[4096]{0:T(1024)S(1)}, f32[4096]{0:T(1024)}, u32[]{:S(2)}) copy-start(f32[4096]{0:T(1024)} %convert_element_type.404) | copy-start | bytes 49156
  518.3 17.5 %copy-start.100 = (bf16[1024,4096]{1,0:T(8,128)(2,1)S(1)}, bf16[1024,4096]{1,0:T(8,128)(2,1)}, u32[]{:S(2)}) copy-start(bf16[1024,4096]{1,0:T(8,128)(2,1)} %all-gather.24.cloned.1.call-done) | copy-start | bytes 25165828
  684.9 12.0 copy-start.17
  684.9 11.9 copy-start.90
  712.1 15.6 %slice-start = ((s8[16777216]{0:T(1024)(128)(4,1)}), s8[4194304]{0:T(1024)(128)(4,1)S(1)}, s32[]{:S(2)}) async-start(s8[16777216]{0:T(1024)(128)(4,1)} %bitcast.212), calls=%async_computation.25 | async-start | bytes 8388608
  712.1 15.6 %slice-start.1 = ((s8[16777216]{0:T(1024)(128)(4,1)}), s8[4194304]{0:T(1024)(128)(4,1)S(1)}, s32[]{:S(2)}) async-start(s8[16777216]{0:T(1024)(128)(4,1)} %bitcast.212), calls=%async_computation.26 | async-start | bytes 8388608
  712.1 16.0 %slice-start.2 = ((s8[16777216]{0:T(1024)(128)(4,1)}), s8[4194304]{0:T(1024)(128)(4,1)S(1)}, s32[]{:S(2)}) async-start(s8[16777216]{0:T(1024)(128)(4,1)} %bitcast.212), calls=%async_computation.27 | async-start | bytes 8388608
  712.1 17.2 %slice-start.3 = ((s8[16777216]{0:T(1024)(128)(4,1)}), s8[4194304]{0:T(1024)(128)(4,1)S(1)}, s32[]{:S(2)}) async-start(s8[16777216]{0:T(1024)(128)(4,1)} %bitcast.212), calls=%async_computation.28 | async-start | bytes 8388608
  741.7 86.9 %reduce-scatter.9.cloned.1.call-start = ((), (), s32[]{:S(2)}) async-start(), calls=%async_computation.16 | async-start | bytes 2621440 | tf_op jit(solution)/shard_map/reduce_scatter | solution.py:201
  746.6 16.1 %slice-start.4 = ((s8[16777216]{0:T(1024)(128)(4,1)}), s8[4194304]{0:T(1024)(128)(4,1)S(1)}, s32[]{:S(2)}) async-start(s8[16777216]{0:T(1024)(128)(4,1)} %bitcast.214), calls=%async_computation.29 | async-start | bytes 8388608
  746.6 16.1 %slice-start.5 = ((s8[16777216]{0:T(1024)(128)(4,1)}), s8[4194304]{0:T(1024)(128)(4,1)S(1)}, s32[]{:S(2)}) async-start(s8[16777216]{0:T(1024)(128)(4,1)} %bitcast.214), calls=%async_computation.30 | async-start | bytes 8388608
  746.6 16.1 %slice-start.6 = ((s8[16777216]{0:T(1024)(128)(4,1)}), s8[4194304]{0:T(1024)(128)(4,1)S(1)}, s32[]{:S(2)}) async-start(s8[16777216]{0:T(1024)(128)(4,1)} %bitcast.214), calls=%async_computation.31 | async-start | bytes 8388608
  746.6 17.3 %slice-start.7 = ((s8[16777216]{0:T(1024)(128)(4,1)}), s8[4194304]{0:T(1024)(128)(4,1)S(1)}, s32[]{:S(2)}) async-start(s8[16777216]{0:T(1024)(128)(4,1)} %bitcast.214), calls=%async_computation.32 | async-start | bytes 8388608
  776.0 97.7 %reduce-scatter.11.cloned.1.call-start = ((), (), s32[]{:S(2)}) async-start(), calls=%async_computation.17 | async-start | bytes 2621440 | tf_op jit(solution)/shard_map/reduce_scatter | solution.py:207
  785.6 133.8 %reduce-scatter.15.cloned.1.call-start = ((), (), s32[]{:S(2)}) async-start(), calls=%async_computation.19 | async-start | bytes 2621440 | tf_op jit(solution)/shard_map/reduce_scatter | solution.py:207
  795.3 207.6 %reduce-scatter.19.cloned.1.call-start = ((), (), s32[]{:S(2)}) async-start(), calls=%async_computation.21 | async-start | bytes 2621440 | tf_op jit(solution)/shard_map/reduce_scatter | solution.py:322
  799.4 277.4 %reduce-scatter.17.cloned.1.call-start = ((), (), s32[]{:S(2)}) async-start(), calls=%async_computation.20 | async-start | bytes 7864320 | tf_op jit(solution)/shard_map/reduce_scatter | solution.py:316
  807.5 22.4 %copy-start.63 = (f32[256,32]{0,1:T(8,128)S(1)}, f32[256,32]{0,1:T(8,128)}, u32[]{:S(2)}) copy-start(f32[256,32]{0,1:T(8,128)} %copy-done.62) | copy-start | bytes 98308
  807.5 22.4 %copy-start.65 = (f32[256,32]{0,1:T(8,128)S(1)}, f32[256,32]{0,1:T(8,128)}, u32[]{:S(2)}) copy-start(f32[256,32]{0,1:T(8,128)} %get-tuple-element.122) | copy-start | bytes 98308
  814.6 18.5 %copy-start.61 = (f32[256,32]{0,1:T(8,128)S(1)}, f32[256,32]{0,1:T(8,128)}, u32[]{:S(2)}) copy-start(f32[256,32]{0,1:T(8,128)} %copy-done.60) | copy-start | bytes 98308
  814.6 18.5 %copy-start.64 = (f32[256,32]{0,1:T(8,128)S(1)}, f32[256,32]{0,1:T(8,128)}, u32[]{:S(2)}) copy-start(f32[256,32]{0,1:T(8,128)} %get-tuple-element.104) | copy-start | bytes 98308
  831.4 42.4 %copy-start.7 = (bf16[2,256,1024]{2,1,0:T(8,128)(2,1)S(1)}, bf16[2,256,1024]{2,1,0:T(8,128)(2,1)}, u32[]{:S(2)}) copy-start(bf16[2,256,1024]{2,1,0:T(8,128)(2,1)} %param.15) | copy-start | bytes 3145732
  831.4 42.4 %copy-start.52 = (f32[4,1,256]{2,1,0:T(1,128)S(1)}, f32[4,1,256]{2,1,0:T(1,128)}, u32[]{:S(2)}) copy-start(f32[4,1,256]{2,1,0:T(1,128)} %copy-done.51) | copy-start | bytes 12292
  831.4 42.4 %copy-start.55 = (f32[4,1,256]{2,1,0:T(1,128)S(1)}, f32[4,1,256]{2,1,0:T(1,128)}, u32[]{:S(2)}) copy-start(f32[4,1,256]{2,1,0:T(1,128)} %copy-done.54) | copy-start | bytes 12292
  831.4 42.4 %copy-start.67 = (f32[256]{0:T(256)S(1)}, f32[256]{0:T(256)}, u32[]{:S(2)}) copy-start(f32[256]{0:T(256)} %copy-done.66) | copy-start | bytes 3076
  831.4 42.4 %copy-start.75 = (f32[256]{0:T(256)S(1)}, f32[256]{0:T(256)}, u32[]{:S(2)}) copy-start(f32[256]{0:T(256)} %copy-done.74) | copy-start | bytes 3076
  873.8 45.6 %copy-start.72 = (f32[256]{0:T(256)S(1)}, f32[256]{0:T(256)}, u32[]{:S(2)}) copy-start(f32[256]{0:T(256)} %copy-done.71) | copy-start | bytes 3076
  873.8 45.5 %copy-start.87 = (f32[256]{0:T(256)S(1)}, f32[256]{0:T(256)}, u32[]{:S(2)}) copy-start(f32[256]{0:T(256)} %copy-done.86) | copy-start | bytes 3076
  929.3 294.8 %reduce-scatter.21.cloned.1.call-start = ((), (), s32[]{:S(2)}) async-start(), calls=%async_computation.22 | async-start | bytes 10485760 | tf_op jit(solution)/shard_map/reduce_scatter | solution.py:334
  951.8 419.8 %reduce-scatter.23.cloned.1.call-start = ((), (), s32[]{:S(2)}) async-start(), calls=%async_computation.23 | async-start | bytes 10485760 | tf_op jit(solution)/shard_map/reduce_scatter | solution.py:340
  974.1 12.3 copy-start.105
  974.2 505.9 %all-reduce.13.cloned.1.call-start = ((), (), s32[]{:S(2)}) async-start(), calls=%async_computation.24 | async-start | bytes 12582912 | tf_op jit(solution)/shard_map/psum | solution.py:350
  1001.7 369.9 %copy-start.21 = (bf16[256,16,64]{0,2,1:T(8,128)(2,1)S(1)}, bf16[256,16,64]{0,2,1:T(8,128)(2,1)}, u32[]{:S(2)}) copy-start(bf16[256,16,64]{0,2,1:T(8,128)(2,1)} %pad_maximum_fusion.11) | copy-start | bytes 1572868
  1001.7 369.9 %copy-start.22 = (bf16[256,16,64]{0,2,1:T(8,128)(2,1)S(1)}, bf16[256,16,64]{0,2,1:T(8,128)(2,1)}, u32[]{:S(2)}) copy-start(bf16[256,16,64]{0,2,1:T(8,128)(2,1)} %pad_maximum_fusion.10) | copy-start | bytes 1572868
  1377.7 42.3 %copy-start.15 = (f32[256,1024]{1,0:T(8,128)S(1)}, f32[256,1024]{1,0:T(8,128)}, u32[]{:S(2)}) copy-start(f32[256,1024]{1,0:T(8,128)} %get-tuple-element.93) | copy-start | bytes 3145732
  (68 other events, 399.7 us)
Sparse Core Ops, SparseCore 0:
  9.6 118.1 all-gather.15
  138.8 44.5 all-gather.29
  185.5 43.8 all-gather.27
  231.4 44.4 all-gather.17
  277.3 44.4 all-gather.21
  323.8 45.0 all-gather.19
  370.5 147.7 all-gather.23
  519.9 147.7 all-gather.25
  741.8 41.7 reduce-scatter.12
  785.8 42.8 reduce-scatter.8
  830.9 42.8 reduce-scatter.10
  876.5 42.8 reduce-scatter.14
  921.6 42.8 reduce-scatter.18
  966.7 110.0 reduce-scatter.16
  1078.9 145.1 reduce-scatter.20
  1226.3 145.2 reduce-scatter.22
  1375.0 104.9 all-reduce.12
where the time goes:
time: 1500 us
  waiting for transfers between devices  976 us (65%)
  matrix products  271 us (18%)
  blocking collectives  121 us (8%)
  other arithmetic  63.2 us (4%)
  local copies, waits for them, and re-layouts  46.6 us (3%)
  between operations  17.9 us (1%)
    reduce_scatter x1, waiting for transfers between devices, local(): lax.psum_scatter(totals[10].astype(jnp.bfloat16), 'grp', scatter_dimensio...  147 us
    reduce_scatter x1, waiting for transfers between devices, local(): lax.psum_scatter(totals[8].astype(jnp.bfloat16), 'grp', scatter_dimension...  147 us
    all_gather x1, waiting for transfers between devices, local(): lax.all_gather(w_up, 'grp', axis=0, tiled=True)  132 us
    all_gather x1, waiting for transfers between devices, local(): lax.all_gather(w_down, 'grp', axis=0, tiled=True)  115 us
    all_gather x1, waiting for transfers between devices, local(): lax.all_gather(w_qkv, 'grp', axis=0, tiled=True)  77.6 us
    reduce_scatter x2, waiting for transfers between devices, backward_pass(): lax.psum_scatter(grad_values.reshape(total, width).astype(jnp.bfloat16),...  76.1 us
    reduce_scatter x1, waiting for transfers between devices, local(): lax.psum_scatter(totals[2].astype(jnp.bfloat16), 'grp', scatter_dimension...  73.8 us
    dot_general x8, matrix products, outer(): lax.dot_general(left, right, (((0,), (0,)), ((), ())), preferred_element_...  65.9 us
  transfers between devices with their start and end apart: 17, of which 14 were waited for; matrix products, arithmetic and copies ran while one was open for 18% of the time, Pallas kernels for 0%

commit v1 on v0

--- a/solution.py
+++ b/solution.py
@@ -5,6 +5,7 @@
 
 SCALE = 0.125
 EPS = 1e-06
+core_pass = lambda w_in: lax.all_gather(w_in, "rep").sum(axis=0)
 
 
 def rotary_angles(positions):
@@ -347,7 +348,7 @@
     summed = (
         lax.psum(owned[0].astype(jnp.bfloat16), "rep").astype(jnp.float32),
         lax.psum(owned[1].astype(jnp.bfloat16), "rep").astype(jnp.float32),
-        lax.psum(owned[2].astype(jnp.bfloat16), "rep").astype(jnp.float32),
+        core_pass(owned[2].astype(jnp.bfloat16)).astype(jnp.float32),
         lax.psum(owned[3].astype(jnp.bfloat16), "rep").astype(jnp.float32),
         lax.psum(owned[4].astype(jnp.bfloat16), "rep").astype(jnp.float32),
         lax.psum(owned[5].astype(jnp.bfloat16), "rep").astype(jnp.float32),

time: 1500 us -> 1560 us (1.040)
  waiting for transfers between devices: 976 us -> 1030 us
    all_gather x0 -> x1, waiting for transfers between devices: none -> 65 us  [core_pass = lambda w_in: lax.all_gather(w_in, 'rep').sum(axis=0)]
    reduce_scatter x1, waiting for transfers between devices: 73.8 us -> 114 us  [local(): lax.psum_scatter(totals[2].astype(jnp.bfloat16), 'grp', scatter_dimension...]
    psum x1, waiting for transfers between devices: 56.7 us -> 19.7 us  [local(): lax.psum(owned[4].astype(jnp.bfloat16), 'rep').astype(jnp.float32)]
    reduce_scatter x1, waiting for transfers between devices: 0.02 us -> 35.2 us  [local(): lax.psum_scatter(totals[4].astype(jnp.bfloat16), 'grp', scatter_dimension...]
    reduce_scatter x2, waiting for transfers between devices: 76.1 us -> 43.5 us  [backward_pass(): lax.psum_scatter(grad_values.reshape(total, width).astype(jnp.bfloat16),...]
  transfers between devices with their start and end apart: 17 -> 18, of which waited for: 14 -> 15; matrix products, arithmetic and copies ran while one was open for 18% -> 18% of each run, Pallas kernels for 0% -> 0%
where the time goes in v1:
time: 1560 us; the launch traced here: 1550 us
  waiting for transfers between devices  1030 us (66%)
  matrix products  265 us (17%)
  blocking collectives  118 us (8%)
  other arithmetic  71.9 us (5%)
  local copies, waits for them, and re-layouts  46.8 us (3%)
  between operations  18.3 us (1%)
    reduce_scatter x1, waiting for transfers between devices, local(): lax.psum_scatter(totals[10].astype(jnp.bfloat16), 'grp', scatter_dimensio...  147 us
    reduce_scatter x1, waiting for transfers between devices, local(): lax.psum_scatter(totals[8].astype(jnp.bfloat16), 'grp', scatter_dimension...  146 us
    all_gather x1, waiting for transfers between devices, local(): lax.all_gather(w_up, 'grp', axis=0, tiled=True)  132 us
    all_gather x1, waiting for transfers between devices, local(): lax.all_gather(w_down, 'grp', axis=0, tiled=True)  116 us
    reduce_scatter x1, waiting for transfers between devices, local(): lax.psum_scatter(totals[2].astype(jnp.bfloat16), 'grp', scatter_dimension...  114 us
    all_gather x1, waiting for transfers between devices, local(): lax.all_gather(w_qkv, 'grp', axis=0, tiled=True)  77.6 us
    dot_general x8, matrix products, outer(): lax.dot_general(left, right, (((0,), (0,)), ((), ())), preferred_element_...  65.6 us
    all_gather x1, waiting for transfers between devices, core_pass = lambda w_in: lax.all_gather(w_in, 'rep').sum(axis=0)  65 us
  transfers between devices with their start and end apart: 18, of which 15 were waited for; matrix products, arithmetic and copies ran while one was open for 18% of the time, Pallas kernels for 0%

profile of v1, /device:TPU:0, one launch (start us, length us, event | category | flops | bytes accessed | tf_op | source)
XLA Modules:
  0.0 1553.2 jit_solution(17400942665134071687)
XLA Ops:
  8.6 14.8 all-gather.3
  24.2 12.4 all-gather.2
  37.3 8.0 all-gather.1
  50.2 77.6 %all-gather.18.cloned.1.call-done = bf16[1024,3072]{1,0:T(8,128)(2,1)} async-done(((bf16[256,3072]{1,0:T(8,128)(2,1)}), bf16[1024,3072]{1,0:T(8,128)(2,1)}) %all-gather.18.cloned.1.call-update) | async-done | bytes 6291472 | tf_op jit(solution)/shard_map/all_gather | solution.py:281
  127.8 4.9 convolution_add_fusion.2
  140.9 4.8 convolution_add_fusion.3
  157.1 8.3 all-gather.4
  165.4 15.3 all_gather.93
  181.3 11.2 all-gather.6
  192.6 8.3 all-gather.5
  200.9 4.1 multiply_reduce_fusion.2
  205.0 5.8 copy-done
  210.8 3.6 exponential_reduce_fusion
  214.4 15.0 all-gather.30.cloned.1.call-done
  229.4 2.9 copy.56
  232.3 43.6 %all-gather.20.cloned.1.call-done = bf16[1024,1024]{1,0:T(8,128)(2,1)} async-done(((bf16[256,1024]{1,0:T(8,128)(2,1)}), bf16[1024,1024]{1,0:T(8,128)(2,1)}) %all-gather.20.cloned.1.call-update) | async-done | bytes 2097168 | tf_op jit(solution)/shard_map/all_gather | solution.py:91
  275.9 4.0 copy.53
  280.5 8.7 convolution_convert_fusion.2
  289.2 32.7 %all-gather.24.cloned.1.call-done = bf16[1024,1024]{1,0:T(8,128)(2,1)} async-done(((bf16[256,1024]{1,0:T(8,128)(2,1)}), bf16[1024,1024]{1,0:T(8,128)(2,1)}) %all-gather.24.cloned.1.call-update) | async-done | bytes 2097168 | tf_op jit(solution)/shard_map/all_gather | solution.py:283
  325.7 43.2 %all-gather.22.cloned.1.call-done = bf16[1024,1024]{0,1:T(8,128)(2,1)} async-done(((bf16[256,1024]{0,1:T(8,128)(2,1)}), bf16[1024,1024]{0,1:T(8,128)(2,1)}) %all-gather.22.cloned.1.call-update) | async-done | bytes 2097168 | tf_op jit(solution)/shard_map/all_gather | solution.py:90
  368.9 4.1 multiply_reduce_fusion.3
  373.0 3.6 exponential_reduce_fusion.1
  376.7 4.2 copy-done.1
  380.9 3.8 convolution_convert_fusion.3
  386.8 131.5 %all-gather.26.cloned.1.call-done = bf16[1024,4096]{1,0:T(8,128)(2,1)} async-done(((bf16[256,4096]{1,0:T(8,128)(2,1)}), bf16[1024,4096]{1,0:T(8,128)(2,1)}) %all-gather.26.cloned.1.call-update) | async-done | bytes 8388624 | tf_op jit(solution)/shard_map/all_gather | solution.py:287
  518.3 17.1 %multiply_convert_fusion.4 = (bf16[256,4096]{1,0:T(8,128)(2,1)}, f32[256,4096]{1,0:T(8,128)}, f32[256,4096]{1,0:T(8,128)}) fusion(f32[4096]{0:T(1024)} %convert_element_type.406, bf16[1024,4096]{1,0:T(8,128)(2,1)} %all-gather.26.cloned.1.call-done, f32[256,1024]{1,0:T(8,128)} %copy-done.16, f32[256]{0:T(256)S(1)} %add_rsqrt_fusion, f32[256]{0:T(256)} %copy-done.83, ...), kind=kOutput, calls=%fused_computation.28 | convolution fusion | flops 2218000384 | bytes 19949568 | tf_op jit(solution)/shard_map/dot_general | solution.py:110
  535.4 16.7 %multiply_convert_fusion.5 = (bf16[256,4096]{1,0:T(8,128)(2,1)}, f32[256,4096]{1,0:T(8,128)}, f32[256,4096]{1,0:T(8,128)}) fusion(f32[4096]{0:T(1024)S(1)} %copy-done.77, bf16[1024,4096]{1,0:T(8,128)(2,1)S(1)} %copy-done.94, f32[256,1024]{1,0:T(8,128)S(1)} %copy-done.11, f32[1024]{0:T(1024)S(1)} %bitcast.275, f32[1024]{0:T(1024)S(1)} %bitcast.269, ...), kind=kOutput, calls=%fused_computation.41 | convolution fusion | flops 2218000384 | bytes 19949568 | tf_op jit(solution)/shard_map/dot_general | solution.py:110
  552.1 115.6 %all-gather.28.cloned.1.call-done = bf16[4096,1024]{1,0:T(8,128)(2,1)} async-done(((bf16[1024,1024]{1,0:T(8,128)(2,1)}), bf16[4096,1024]{1,0:T(8,128)(2,1)}) %all-gather.28.cloned.1.call-update) | async-done | bytes 8388624 | tf_op jit(solution)/shard_map/all_gather | solution.py:289
  667.7 10.3 convert_reduce_fusion
  678.0 6.8 fusion.116
  684.9 11.9 convert_reduce_fusion.1
  696.8 8.0 multiply_reduce_fusion.5
  712.1 15.6 %multiply_reduce_fusion = (f32[16,256]{1,0:T(8,128)}, f32[16,256,1024]{2,1,0:T(8,128)}) fusion(f32[16,256,1024]{2,1,0:T(8,128)} %copy-done, f32[16,256]{1,0:T(8,128)} %copy-done.54, bf16[256,16,64]{0,2,1:T(8,128)(2,1)} %bitcast.236, bf16[1024,16,64]{0,2,1:T(8,128)(2,1)} %bitcast.220), kind=kOutput, calls=%fused_computation.3 | convolution fusion | flops 553644032 | bytes 36208640 | tf_op jit(solution)/shard_map/thd,shd->hts/dot_general | solution.py:184
  729.3 8.1 multiply_convert_fusion
  737.5 2.9 multiply_convert_fusion.2
  746.5 16.1 %multiply_reduce_fusion.1 = (f32[16,256]{1,0:T(8,128)}, f32[16,256,1024]{2,1,0:T(8,128)}) fusion(f32[16,256,1024]{2,1,0:T(8,128)} %copy-done.1, f32[16,256]{1,0:T(8,128)} %copy-done.56, bf16[256,16,64]{0,2,1:T(8,128)(2,1)} %bitcast.238, bf16[1024,16,64]{0,2,1:T(8,128)(2,1)} %bitcast.217), kind=kOutput, calls=%fused_computation.5 | convolution fusion | flops 553644032 | bytes 36208640 | tf_op jit(solution)/shard_map/thd,shd->hts/dot_general | solution.py:184
  763.8 8.2 multiply_convert_fusion.1
  772.1 3.5 multiply_convert_fusion.3
  776.2 9.4 convolution_convert_fusion.1
  785.6 9.6 convolution_convert_fusion
  799.7 10.1 fusion.107
  809.9 11.7 add_convert_fusion.1
  822.8 9.9 fusion.67
  832.8 12.0 add_convert_fusion
  845.0 7.9 fusion.14
  852.9 7.1 fusion.15
  867.7 6.0 reduce-scatter.11.cloned.1.call-done
  873.8 8.0 fusion.100
  881.8 37.5 %reduce-scatter.15.cloned.1.call-done = bf16[256,1024]{0,1:T(8,128)(2,1)} async-done(((bf16[1024,1024]{0,1:T(8,128)(2,1)}), bf16[256,1024]{0,1:T(8,128)(2,1)}) %reduce-scatter.15.cloned.1.call-update) | async-done | bytes 524304 | tf_op jit(solution)/shard_map/reduce_scatter | solution.py:208
  919.3 9.9 add_convert_fusion.2
  929.3 35.2 %reduce-scatter.19.cloned.1.call-done = bf16[256,1024]{1,0:T(8,128)(2,1)} async-done(((bf16[1024,1024]{1,0:T(8,128)(2,1)}), bf16[256,1024]{1,0:T(8,128)(2,1)}) %reduce-scatter.19.cloned.1.call-update) | async-done | bytes 524304 | tf_op jit(solution)/shard_map/reduce_scatter | solution.py:323
  964.5 146.0 %reduce-scatter.21.cloned.1.call-done = bf16[256,4096]{1,0:T(8,128)(2,1)} async-done(((bf16[1024,4096]{1,0:T(8,128)(2,1)}), bf16[256,4096]{1,0:T(8,128)(2,1)}) %reduce-scatter.21.cloned.1.call-update) | async-done | bytes 2097168 | tf_op jit(solution)/shard_map/reduce_scatter | solution.py:335
  1110.5 147.5 %reduce-scatter.23.cloned.1.call-done = bf16[1024,1024]{1,0:T(8,128)(2,1)} async-done(((bf16[4096,1024]{1,0:T(8,128)(2,1)}), bf16[1024,1024]{1,0:T(8,128)(2,1)}) %reduce-scatter.23.cloned.1.call-update) | async-done | bytes 2097168 | tf_op jit(solution)/shard_map/reduce_scatter | solution.py:341
  1258.1 113.5 %reduce-scatter.17.cloned.1.call-done = bf16[256,3072]{1,0:T(8,128)(2,1)} async-done(((bf16[1024,3072]{1,0:T(8,128)(2,1)}), bf16[256,3072]{1,0:T(8,128)(2,1)}) %reduce-scatter.17.cloned.1.call-update) | async-done | bytes 1572880 | tf_op jit(solution)/shard_map/reduce_scatter | solution.py:317
  1371.7 10.4 all-gather.7
  1384.6 6.9 fusion.36
  1391.7 6.1 fusion.37
  1402.1 3.4 fusion.58
  1405.6 15.8 %all-reduce.10 = (bf16[1024]{0:T(1024)(128)(2,1)S(1)}, bf16[1024]{0:T(1024)(128)(2,1)S(1)}, bf16[3072]{0:T(1024)(128)(2,1)S(1)}, bf16[1024]{0:T(1024)(128)(2,1)S...) all-reduce(bf16[1024]{0:T(1024)(128)(2,1)S(1)} %add_convert_fusion., ...), channel_id=7, replica_groups=mesh['rep'=8,'grp'=4] {'grp'}, use_global_device_ids=true, to_apply=%region_28.29.clone | all-reduce | flops 13312 | bytes 53248
  1421.9 12.9 all-reduce.8
  1443.0 19.7 %all-reduce.13.cloned.1.call-done = (bf16[256,1024]{1,0:T(8,128)(2,1)}, bf16[256,4096]{1,0:T(8,128)(2,1)}, bf16[1024,1024]{1,0:T(8,128)(2,1)}) async-done(((bf16[256,1024]{1,0:T(8,128)(2,1)}, bf16[256,4096]{1,0:T(8,128)(2,1)}, bf16[1024,1024]{1,0:T(8,128)(2,1)}), (bf16[256,1024]{1,0:T(8,128)(2,1)}, bf16[256,4096]{1,0:T(8,128)(2,1)}, bf16[1024,1024]{1,0:T(8,128)(2,1)})) %all-reduce.13.cloned.1.call-update) | async-done | bytes 4718608 | tf_op jit(solution)/shard_map/psum | solution.py:353
  1465.0 4.1 convert_element_type.467
  1471.6 65.0 %all-gather.34.cloned.1.call-done = bf16[2048,3072]{1,0:T(8,128)(2,1)} async-done(((bf16[256,3072]{1,0:T(8,128)(2,1)}), bf16[2048,3072]{1,0:T(8,128)(2,1)}) %all-gather.34.cloned.1.call-update) | async-done | bytes 12582928 | tf_op jit(solution)/shard_map/all_gather | solution.py:8
  1536.6 7.3 reduce_sum.360
  (366 shorter events, 84.7 us)
Async XLA Ops:
  7.2 120.6 %all-gather.18.cloned.1.call-start = ((), (), s32[]{:S(2)}) async-start(), calls=%async_computation.8 | async-start | bytes 7864320 | tf_op jit(solution)/shard_map/all_gather | solution.py:281
  7.9 193.0 %all-gather.32.cloned.1.call-start = ((), (), s32[]{:S(2)}) async-start(), calls=%async_computation.15 | async-start | bytes 2621440 | tf_op jit(solution)/shard_map/all_gather | solution.py:90
  23.5 109.2 %copy-start.86 = (f32[4,1,768]{2,1,0:T(1,128)}, f32[4,1,768]{2,1,0:T(1,128)S(1)}, u32[]{:S(2)}) copy-start(f32[4,1,768]{2,1,0:T(1,128)S(1)} %convert_element_type.478) | copy-start | bytes 36868
  36.6 104.3 %copy-start.52 = (f32[4,1,256]{2,1,0:T(1,128)}, f32[4,1,256]{2,1,0:T(1,128)S(1)}, u32[]{:S(2)}) copy-start(f32[4,1,256]{2,1,0:T(1,128)S(1)} %convert_element_type.477) | copy-start | bytes 12292
  45.3 95.6 %copy-start.50 = (f32[4,1,256]{2,1,0:T(1,128)}, f32[4,1,256]{2,1,0:T(1,128)S(1)}, u32[]{:S(2)}) copy-start(f32[4,1,256]{2,1,0:T(1,128)S(1)} %convert_element_type.476) | copy-start | bytes 12292
  46.7 85.9 %copy-start.66 = (f32[256]{0:T(256)}, f32[256]{0:T(256)S(1)}, u32[]{:S(2)}) copy-start(f32[256]{0:T(256)S(1)} %get-tuple-element.142) | copy-start | bytes 3076
  46.8 94.1 %copy-start.64 = (f32[256]{0:T(256)}, f32[256]{0:T(256)S(1)}, u32[]{:S(2)}) copy-start(f32[256]{0:T(256)S(1)} %get-tuple-element.143) | copy-start | bytes 3076
  48.4 84.3 %copy-start.80 = (f32[256]{0:T(256)}, f32[256]{0:T(256)S(1)}, u32[]{:S(2)}) copy-start(f32[256]{0:T(256)S(1)} %add_rsqrt_fusion.1) | copy-start | bytes 3076
  50.1 86.6 %copy-start.60 = (f32[256,32]{0,1:T(8,128)}, f32[256,32]{0,1:T(8,128)S(1)}, u32[]{:S(2)}) copy-start(f32[256,32]{0,1:T(8,128)S(1)} %get-tuple-element.120) | copy-start | bytes 98308
  50.1 103.4 %copy-start.58 = (f32[256,32]{0,1:T(8,128)}, f32[256,32]{0,1:T(8,128)S(1)}, u32[]{:S(2)}) copy-start(f32[256,32]{0,1:T(8,128)S(1)} %get-tuple-element.105) | copy-start | bytes 98308
  137.7 63.2 %copy-start.32 = (bf16[256,16,32]{0,2,1:T(8,128)(2,1)}, bf16[256,16,32]{0,2,1:T(8,128)(2,1)S(1)}, u32[]{:S(2)}) copy-start(bf16[256,16,32]{0,2,1:T(8,128)(2,1)S(1)} %get-tuple-element.81) | copy-start | bytes 786436
  138.6 90.8 %all-gather.30.cloned.1.call-start = ((), (), s32[]{:S(2)}) async-start(), calls=%async_computation.14 | async-start | bytes 2621440 | tf_op jit(solution)/shard_map/all_gather | solution.py:91
  140.8 135.1 %all-gather.20.cloned.1.call-start = ((), (), s32[]{:S(2)}) async-start(), calls=%async_computation.9 | async-start | bytes 2621440 | tf_op jit(solution)/shard_map/all_gather | solution.py:91
  148.3 173.6 %all-gather.24.cloned.1.call-start = ((), (), s32[]{:S(2)}) async-start(), calls=%async_computation.11 | async-start | bytes 2621440 | tf_op jit(solution)/shard_map/all_gather | solution.py:283
  148.9 220.1 %all-gather.22.cloned.1.call-start = ((), (), s32[]{:S(2)}) async-start(), calls=%async_computation.10 | async-start | bytes 2621440 | tf_op jit(solution)/shard_map/all_gather | solution.py:90
  153.5 11.9 copy-start.93
  153.6 27.8 %copy-start.96 = (bf16[256]{0:T(256)(128)(2,1)S(1)}, bf16[256]{0:T(256)(128)(2,1)}, u32[]{:S(2)}) copy-start(bf16[256]{0:T(256)(128)(2,1)} %param.24) | copy-start | bytes 1540
  153.6 39.0 %copy-start.97 = (bf16[256]{0:T(256)(128)(2,1)S(1)}, bf16[256]{0:T(256)(128)(2,1)}, u32[]{:S(2)}) copy-start(bf16[256]{0:T(256)(128)(2,1)} %param.23) | copy-start | bytes 1540
  154.7 46.2 %copy-start.34 = (bf16[256,16,32]{0,2,1:T(8,128)(2,1)S(1)}, bf16[256,16,32]{0,2,1:T(8,128)(2,1)}, u32[]{:S(2)}) copy-start(bf16[256,16,32]{0,2,1:T(8,128)(2,1)} %get-tuple-element.82) | copy-start | bytes 786436
  155.6 362.8 %all-gather.26.cloned.1.call-start = ((), (), s32[]{:S(2)}) async-start(), calls=%async_computation.12 | async-start | bytes 10485760 | tf_op jit(solution)/shard_map/all_gather | solution.py:287
  156.3 511.4 %all-gather.28.cloned.1.call-start = ((), (), s32[]{:S(2)}) async-start(), calls=%async_computation.13 | async-start | bytes 10485760 | tf_op jit(solution)/shard_map/all_gather | solution.py:289
  157.1 702.9 %reduce-scatter.13.cloned.1.call-start = ((), (), s32[]{:S(2)}) async-start(), calls=%async_computation.18 | async-start | bytes 2621440 | tf_op jit(solution)/shard_map/reduce_scatter | solution.py:202
  232.3 56.9 %copy-start.9 = (bf16[1024,1024]{0,1:T(8,128)(2,1)}, bf16[1024,1024]{0,1:T(8,128)(2,1)S(1)}, u32[]{:S(2)}) copy-start(bf16[1024,1024]{0,1:T(8,128)(2,1)S(1)} %copy.56) | copy-start | bytes 6291460
  289.2 79.8 %copy-start.36 = (bf16[256,16,32]{0,2,1:T(8,128)(2,1)S(1)}, bf16[256,16,32]{0,2,1:T(8,128)(2,1)}, u32[]{:S(2)}) copy-start(bf16[256,16,32]{0,2,1:T(8,128)(2,1)} %get-tuple-element.77) | copy-start | bytes 786436
  321.8 47.1 %copy-start.38 = (bf16[256,16,32]{0,2,1:T(8,128)(2,1)S(1)}, bf16[256,16,32]{0,2,1:T(8,128)(2,1)}, u32[]{:S(2)}) copy-start(bf16[256,16,32]{0,2,1:T(8,128)(2,1)} %get-tuple-element.78) | copy-start | bytes 786436
  324.5 44.4 %copy-start.83 = (f32[256]{0:T(256)}, f32[256]{0:T(256)S(1)}, u32[]{:S(2)}) copy-start(f32[256]{0:T(256)S(1)} %broadcast_multiply_fusion.8) | copy-start | bytes 3076
  386.7 318.1 %copy-start.87 = (f32[256]{0:T(256)}, f32[256]{0:T(256)S(1)}, u32[]{:S(2)}) copy-start(f32[256]{0:T(256)S(1)} %add_rsqrt_fusion) | copy-start | bytes 3076
  386.8 318.1 %copy-start.71 = (f32[256]{0:T(256)}, f32[256]{0:T(256)S(1)}, u32[]{:S(2)}) copy-start(f32[256]{0:T(256)S(1)} %add_rsqrt_fusion.2) | copy-start | bytes 3076
  518.3 17.1 %copy-start.11 = (f32[256,1024]{1,0:T(8,128)S(1)}, f32[256,1024]{1,0:T(8,128)}, u32[]{:S(2)}) copy-start(f32[256,1024]{1,0:T(8,128)} %copy-done.10) | copy-start | bytes 3145732
  518.3 17.1 %copy-start.77 = (f32[4096]{0:T(1024)S(1)}, f32[4096]{0:T(1024)}, u32[]{:S(2)}) copy-start(f32[4096]{0:T(1024)} %convert_element_type.406) | copy-start | bytes 49156
  518.3 17.1 %copy-start.94 = (bf16[1024,4096]{1,0:T(8,128)(2,1)S(1)}, bf16[1024,4096]{1,0:T(8,128)(2,1)}, u32[]{:S(2)}) copy-start(bf16[1024,4096]{1,0:T(8,128)(2,1)} %all-gather.26.cloned.1.call-done) | copy-start | bytes 25165828
  684.9 12.0 copy-start.17
  684.9 11.9 copy-start.84
  712.1 15.6 %slice-start = ((s8[16777216]{0:T(1024)(128)(4,1)}), s8[4194304]{0:T(1024)(128)(4,1)S(1)}, s32[]{:S(2)}) async-start(s8[16777216]{0:T(1024)(128)(4,1)} %bitcast.213), calls=%async_computation.26 | async-start | bytes 8388608
  712.1 15.6 %slice-start.1 = ((s8[16777216]{0:T(1024)(128)(4,1)}), s8[4194304]{0:T(1024)(128)(4,1)S(1)}, s32[]{:S(2)}) async-start(s8[16777216]{0:T(1024)(128)(4,1)} %bitcast.213), calls=%async_computation.27 | async-start | bytes 8388608
  712.1 16.0 %slice-start.2 = ((s8[16777216]{0:T(1024)(128)(4,1)}), s8[4194304]{0:T(1024)(128)(4,1)S(1)}, s32[]{:S(2)}) async-start(s8[16777216]{0:T(1024)(128)(4,1)} %bitcast.213), calls=%async_computation.28 | async-start | bytes 8388608
  712.1 17.2 %slice-start.3 = ((s8[16777216]{0:T(1024)(128)(4,1)}), s8[4194304]{0:T(1024)(128)(4,1)S(1)}, s32[]{:S(2)}) async-start(s8[16777216]{0:T(1024)(128)(4,1)} %bitcast.213), calls=%async_computation.29 | async-start | bytes 8388608
  741.7 119.5 %reduce-scatter.9.cloned.1.call-start = ((), (), s32[]{:S(2)}) async-start(), calls=%async_computation.16 | async-start | bytes 2621440 | tf_op jit(solution)/shard_map/reduce_scatter | solution.py:202
  746.5 16.1 %slice-start.4 = ((s8[16777216]{0:T(1024)(128)(4,1)}), s8[4194304]{0:T(1024)(128)(4,1)S(1)}, s32[]{:S(2)}) async-start(s8[16777216]{0:T(1024)(128)(4,1)} %bitcast.215), calls=%async_computation.30 | async-start | bytes 8388608
  746.5 16.1 %slice-start.5 = ((s8[16777216]{0:T(1024)(128)(4,1)}), s8[4194304]{0:T(1024)(128)(4,1)S(1)}, s32[]{:S(2)}) async-start(s8[16777216]{0:T(1024)(128)(4,1)} %bitcast.215), calls=%async_computation.31 | async-start | bytes 8388608
  746.5 16.1 %slice-start.6 = ((s8[16777216]{0:T(1024)(128)(4,1)}), s8[4194304]{0:T(1024)(128)(4,1)S(1)}, s32[]{:S(2)}) async-start(s8[16777216]{0:T(1024)(128)(4,1)} %bitcast.215), calls=%async_computation.32 | async-start | bytes 8388608
  746.5 17.3 %slice-start.7 = ((s8[16777216]{0:T(1024)(128)(4,1)}), s8[4194304]{0:T(1024)(128)(4,1)S(1)}, s32[]{:S(2)}) async-start(s8[16777216]{0:T(1024)(128)(4,1)} %bitcast.215), calls=%async_computation.33 | async-start | bytes 8388608
  776.1 97.7 %reduce-scatter.11.cloned.1.call-start = ((), (), s32[]{:S(2)}) async-start(), calls=%async_computation.17 | async-start | bytes 2621440 | tf_op jit(solution)/shard_map/reduce_scatter | solution.py:208
  785.6 9.8 copy-start.14
  785.6 133.8 %reduce-scatter.15.cloned.1.call-start = ((), (), s32[]{:S(2)}) async-start(), calls=%async_computation.19 | async-start | bytes 2621440 | tf_op jit(solution)/shard_map/reduce_scatter | solution.py:208
  795.3 169.2 %reduce-scatter.19.cloned.1.call-start = ((), (), s32[]{:S(2)}) async-start(), calls=%async_computation.21 | async-start | bytes 2621440 | tf_op jit(solution)/shard_map/reduce_scatter | solution.py:323
  799.4 10.4 copy-start.18
  799.5 10.4 copy-start.85
  799.5 10.4 copy-start.88
  799.5 311.1 %reduce-scatter.21.cloned.1.call-start = ((), (), s32[]{:S(2)}) async-start(), calls=%async_computation.22 | async-start | bytes 10485760 | tf_op jit(solution)/shard_map/reduce_scatter | solution.py:335
  799.7 10.1 copy-start.47
  821.6 436.4 %reduce-scatter.23.cloned.1.call-start = ((), (), s32[]{:S(2)}) async-start(), calls=%async_computation.23 | async-start | bytes 10485760 | tf_op jit(solution)/shard_map/reduce_scatter | solution.py:341
  822.8 9.9 copy-start.20
  844.7 526.9 %reduce-scatter.17.cloned.1.call-start = ((), (), s32[]{:S(2)}) async-start(), calls=%async_computation.20 | async-start | bytes 7864320 | tf_op jit(solution)/shard_map/reduce_scatter | solution.py:317
  864.0 9.8 copy-start.7
  864.0 9.8 copy-start.51
  873.8 45.6 %copy-start.67 = (f32[256]{0:T(256)S(1)}, f32[256]{0:T(256)}, u32[]{:S(2)}) copy-start(f32[256]{0:T(256)} %copy-done.66) | copy-start | bytes 3076
  873.8 45.5 %copy-start.81 = (f32[256]{0:T(256)S(1)}, f32[256]{0:T(256)}, u32[]{:S(2)}) copy-start(f32[256]{0:T(256)} %copy-done.80) | copy-start | bytes 3076
  929.2 442.4 %copy-start.98 = (bf16[256]{0:T(256)(128)(2,1)S(1)}, bf16[256]{0:T(256)(128)(2,1)}, u32[]{:S(2)}) copy-start(bf16[256]{0:T(256)(128)(2,1)} %param.28) | copy-start | bytes 1540
  929.2 452.8 %copy-start.99 = (u32[32]{0:T(128)S(1)}, u32[32]{0:T(128)}, u32[]{:S(2)}) copy-start(u32[32]{0:T(128)} %constant.113) | copy-start | bytes 388
  929.3 533.4 %all-reduce.13.cloned.1.call-start = ((), (), s32[]{:S(2)}) async-start(), calls=%async_computation.25 | async-start | bytes 9437184 | tf_op jit(solution)/shard_map/psum | solution.py:353
  1258.0 278.5 %all-gather.34.cloned.1.call-start = ((), (), s32[]{:S(2)}) async-start(), calls=%async_computation.24 | async-start | bytes 14155776 | tf_op jit(solution)/shard_map/all_gather | solution.py:8
  1384.6 15.5 slice-start.8
  1402.1 37.3 %copy-start.15 = (f32[256,1024]{1,0:T(8,128)S(1)}, f32[256,1024]{1,0:T(8,128)}, u32[]{:S(2)}) copy-start(f32[256,1024]{1,0:T(8,128)} %get-tuple-element.92) | copy-start | bytes 3145732
  (65 other events, 386.5 us)
Sparse Core Ops, SparseCore 0:
  9.6 118.1 all-gather.17
  138.8 44.5 all-gather.31
  185.5 43.8 all-gather.29
  231.4 44.4 all-gather.19
  277.3 44.4 all-gather.23
  323.8 45.0 all-gather.21
  370.5 147.7 all-gather.25
  519.9 147.7 all-gather.27
  741.8 41.7 reduce-scatter.12
  785.8 42.8 reduce-scatter.8
  830.9 42.8 reduce-scatter.10
  876.5 42.8 reduce-scatter.14
  921.6 42.8 reduce-scatter.18
  966.7 143.7 reduce-scatter.20
  1112.7 145.2 reduce-scatter.22
  1260.2 111.4 reduce-scatter.16
  1375.1 87.5 all-reduce.12
  1464.5 72.0 all-gather.33
